TPU v7x, 32 devices: a whole 2x2x4 slice. The times are simulated.
32 devices in a mesh: grp: 4 (over x, core), mem: 8 (over z, y).
Axes of the slice: x: 2, y: 2, z: 4, core: 2. Of those that a mesh axis runs over, the one named last changes fastest.
Arguments:
- amplitudes: bfloat16 [384, 262144], P('mem', 'grp'), may hold values from -6 to 6
- integrals: bfloat16 [262144, 1024], P(('grp', 'mem')), may hold values from -0.0625 to 0.0625
- irrep_ef: int32 [262144], P(('grp', 'mem')), may hold values from 0 to 7
- irrep_ab: int32 [1024], replicated, may hold values from 0 to 7
Outputs:
- residual: float32 [384, 1024], P('mem', 'grp')
All inputs are finite; a program needn't handle non-finite values.
Results may differ from a plain program's by a relative error of at most 0.0003.
Values may be sent and summed in bfloat16 or wider, within the bound.
No kernel may reach another device: no remote copies, remote signals or barrier semaphores. Data moves between devices by JAX's collectives and lax.ppermute only.
A program may use at most 128 MiB of HBM per device.

v0:
```python
import jax
import jax.numpy as jnp
from jax import lax
from jax.sharding import PartitionSpec as P


def local(amplitudes, integrals, irrep_ef, irrep_ab):
    member_count = lax.axis_size("mem")
    own_rows = amplitudes.shape[0]
    pair_cols = integrals.shape[0]
    allowed = irrep_ef[:, None] == irrep_ab[None, :]
    blocked = jnp.where(allowed, integrals, jnp.zeros_like(integrals))
    shaped = amplitudes.reshape(own_rows, member_count, pair_cols)
    arrived = lax.all_to_all(shaped, "mem", split_axis=1, concat_axis=0, tiled=True)
    partial_value = jnp.dot(
        arrived.reshape(-1, pair_cols), blocked, preferred_element_type=jnp.float32
    )
    row_share = lax.psum_scatter(partial_value, "mem", scatter_dimension=0, tiled=True)
    result = lax.psum_scatter(row_share, "grp", scatter_dimension=1, tiled=True)
    return result


def solution(mesh):
    placed = (P("mem", "grp"), P(("grp", "mem"), None), P(("grp", "mem")), P())
    return jax.shard_map(
        local, mesh=mesh, in_specs=placed, out_specs=P("mem", "grp"), check_vma=False
    )
```

profile of v0, /device:TPU:0, one launch (start us, length us, event | category | flops | bytes accessed | tf_op | source)
XLA Modules:
  0.0 271.0 jit_solution(445686489094129673)
XLA Ops:
  6.5 0.0 reduce-scatter.7.cloned.1.call-start
  6.5 3.2 %copy.15 = bf16[6,8,8,8192]{3,2,0,1:T(8,128)(2,1)S(1)} copy(bf16[6,8,8,8192]{3,2,1,0:T(8,128)(2,1)} %bitcast.14) | data formatting | bytes 12582912 | tf_op jit(solution)/shard_map/reshape | solution.py:13
  9.7 0.0 copy-start
  9.7 0.0 copy-start.1
  9.8 145.3 %all_to_all.15 = bf16[48,8,8192]{2,0,1:T(8,128)(2,1)} all-to-all(bf16[48,8,8192]{2,0,1:T(8,128)(2,1)S(1)} %bitcast.13), channel_id=1, replica_groups=mesh['grp'=4,'mem'=8] {'mem'}, dimensions={1} | all-to-all | bytes 12582912 | tf_op jit(solution)/shard_map/all_to_all | solution.py:14
  155.1 0.0 copy-done
  155.1 0.0 copy-done.1
  155.1 17.7 %fusion.4 = f32[384,1024]{0,1:T(8,128)S(1)} fusion(bf16[384,8192]{1,0:T(8,128)(2,1)} %bitcast.15, bf16[8192,1024]{1,0:T(8,128)(2,1)} %param.5, s32[1024]{0:T(1024)S(1)} %copy-done.1, s32[8192]{0:T(1024)S(1)} %copy-done), kind=kOutput, calls=%fused_computation.6 | convolution fusion | flops 6459228160 | bytes 24678400 | tf_op jit(solution)/shard_map/dot_general | solution.py:15
  172.8 1.6 copy.11
  174.4 0.0 reduce-scatter.7.cloned.1.call-update
  174.5 0.0 reduce-scatter.5.cloned.1.call-start
  174.5 65.1 %reduce-scatter.7.cloned.1.call-done = f32[48,1024]{1,0:T(8,128)} async-done(((f32[384,1024]{1,0:T(8,128)}), f32[48,1024]{1,0:T(8,128)}) %reduce-scatter.7.cloned.1.call-update) | async-done | bytes 196624
  239.6 1.9 copy.12
  241.5 0.0 reduce-scatter.5.cloned.1.call-update
  241.5 21.0 %reduce-scatter.5.cloned.1.call-done = f32[48,256]{0,1:T(8,128)} async-done(((f32[48,1024]{0,1:T(8,128)}), f32[48,256]{0,1:T(8,128)}) %reduce-scatter.5.cloned.1.call-update) | async-done | bytes 49168 | tf_op jit(solution)/shard_map/reduce_scatter | solution.py:19
  262.5 1.6 copy.10
Async XLA Ops:
  6.5 233.0 %reduce-scatter.7.cloned.1.call-start = ((), (), s32[]{:S(2)}) async-start(), calls=%async_computation.4 | async-start | bytes 1769472
  9.7 145.4 %copy-start = (s32[8192]{0:T(1024)S(1)}, s32[8192]{0:T(1024)}, u32[]{:S(2)}) copy-start(s32[8192]{0:T(1024)} %param.6) | copy-start | bytes 98308
  9.7 145.3 %copy-start.1 = (s32[1024]{0:T(1024)S(1)}, s32[1024]{0:T(1024)}, u32[]{:S(2)}) copy-start(s32[1024]{0:T(1024)} %param.7) | copy-start | bytes 12292
  174.5 88.1 %reduce-scatter.5.cloned.1.call-start = ((), (), s32[]{:S(2)}) async-start(), calls=%async_computation.3 | async-start | bytes 655360 | tf_op jit(solution)/shard_map/reduce_scatter | solution.py:19
Sparse Core Ops, SparseCore 0:
  174.6 64.9 reduce-scatter.6
  242.1 20.4 reduce-scatter.4
where the time goes:
time: 271 us
  blocking collectives  145 us (54%)
  waiting for transfers between devices  86.1 us (32%)
  matrix products  17.7 us (7%)
  between operations  13.4 us (5%)
  local copies, waits for them, and re-layouts  8.38 us (3%)
    all_to_all x1, blocking collectives, local(): lax.all_to_all(shaped, 'mem', split_axis=1, concat_axis=0, tiled=True)  145 us
    unnamed x3, waiting for transfers between devices  65.1 us
    reduce_scatter x1, waiting for transfers between devices, local(): result = lax.psum_scatter(row_share, 'grp', scatter_dimension=1, tiled=True)  21 us
    dot_general x1, matrix products, local(): jnp.dot(arrived.reshape(-1, pair_cols), blocked, preferred_element_type=j...  17.7 us
  transfers between devices with their start and end apart: 2, of which 2 were waited for; matrix products, arithmetic and copies ran while one was open for 0% of the time, Pallas kernels for 0%

commit v1 on v0

--- a/solution.py
+++ b/solution.py
@@ -11,7 +11,10 @@
     allowed = irrep_ef[:, None] == irrep_ab[None, :]
     blocked = jnp.where(allowed, integrals, jnp.zeros_like(integrals))
     shaped = amplitudes.reshape(own_rows, member_count, pair_cols)
-    arrived = lax.all_to_all(shaped, "mem", split_axis=1, concat_axis=0, tiled=True)
+    arrived = jnp.concatenate(
+        lax.all_to_all(jnp.stack(jnp.split(shaped, lax.axis_size("mem"), axis=1)), "mem", 0, 0),
+        axis=0,
+    )
     partial_value = jnp.dot(
         arrived.reshape(-1, pair_cols), blocked, preferred_element_type=jnp.float32
     )

time: 271 us -> 281 us (1.037)
  local copies, waits for them, and re-layouts: 8.38 us -> 27.7 us
  matrix products: 17.7 us -> 8.16 us
    unnamed x3 -> x2, waiting for transfers between devices: 65.1 us -> 0.03 us
    reduce_scatter x0 -> x1, waiting for transfers between devices: none -> 64.6 us  [local(): lax.psum_scatter(partial_value, 'mem', scatter_dimension=0, tiled=True)]
    split x0 -> x1, local copies, waits for them, and re-layouts: none -> 14.5 us  [local(): jnp.split(shaped, lax.axis_size('mem'), axis=1)]
    dot_general x1, matrix products: 17.7 us -> 8.16 us  [local(): jnp.dot(arrived.reshape(-1, pair_cols), blocked, preferred_element_type=j...]
    unnamed x6 -> x20, local copies, waits for them, and re-layouts: 3.58 us -> 12.3 us
    reshape x1 -> x0, local copies, waits for them, and re-layouts: 3.19 us -> none  [local(): shaped = amplitudes.reshape(own_rows, member_count, pair_cols)]
where the time goes in v1:
time: 281 us
  blocking collectives  145 us (52%)
  waiting for transfers between devices  85.7 us (30%)
  local copies, waits for them, and re-layouts  27.7 us (10%)
  between operations  13.6 us (5%)
  matrix products  8.16 us (3%)
    all_to_all x1, blocking collectives, local(): lax.all_to_all(jnp.stack(jnp.split(shaped, lax.axis_size('mem'), axis=1))...  145 us
    reduce_scatter x1, waiting for transfers between devices, local(): lax.psum_scatter(partial_value, 'mem', scatter_dimension=0, tiled=True)  64.6 us
    reduce_scatter x1, waiting for transfers between devices, local(): result = lax.psum_scatter(row_share, 'grp', scatter_dimension=1, tiled=True)  21 us
    split x1, local copies, waits for them, and re-layouts, local(): jnp.split(shaped, lax.axis_size('mem'), axis=1)  14.5 us
    unnamed x20, local copies, waits for them, and re-layouts  12.3 us
    dot_general x1, matrix products, local(): jnp.dot(arrived.reshape(-1, pair_cols), blocked, preferred_element_type=j...  8.16 us
  transfers between devices with their start and end apart: 2, of which 2 were waited for; matrix products, arithmetic and copies ran while one was open for 0% of the time, Pallas kernels for 0%

profile of v1, /device:TPU:0, one launch (start us, length us, event | category | flops | bytes accessed | tf_op | source)
XLA Modules:
  0.0 280.6 jit_solution(3707344732023109267)
XLA Ops:
  6.5 6.2 %copy.41 = bf16[6,8,8,8192]{3,2,1,0:T(8,128)(2,1)S(1)} copy(bf16[6,8,8,8192]{3,1,2,0:T(8,128)(2,1)} %bitcast.21) | data formatting | bytes 12582912
  12.8 14.5 %fusion.5 = (bf16[48,1,8192]{2,1,0:T(2,128)(2,1)S(1)}, bf16[48,1,8192]{2,1,0:T(2,128)(2,1)S(1)}, bf16[48,1,8192]{2,1,0:T(2,128)(2,1)S(1)}, bf16[48,1,8192]{2,1,0...) fusion(bf16[48,8,8192]{2,1,0:T(8,128)(2,1)S(1)} %bitcast.20), kind=kLoop, calls=%fused_computation.14 | loop fusion | bytes 12582912 | tf_op jit(solution)/shard_map/split | solution.py:15
  27.3 0.0 slice-start
  27.3 0.9 bitcast_dynamic-update-slice_fusion.7
  28.2 0.9 bitcast_dynamic-update-slice_fusion.6
  29.0 0.9 bitcast_dynamic-update-slice_fusion.5
  29.9 0.0 slice-start.1
  29.9 0.9 bitcast_dynamic-update-slice_fusion.4
  30.8 0.9 bitcast_dynamic-update-slice_fusion.3
  31.7 0.9 bitcast_dynamic-update-slice_fusion.2
  32.5 0.0 slice-start.2
  32.5 0.9 bitcast_dynamic-update-slice_fusion.1
  33.4 0.9 bitcast_dynamic-update-slice_fusion
  34.3 0.0 slice-start.3
  34.3 0.0 copy-start
  34.3 0.0 copy-start.1
  34.3 145.5 %all_to_all.5 = bf16[8,48,1,8192]{3,1,2,0:T(8,128)(2,1)S(1)} all-to-all(bf16[8,48,1,8192]{3,1,2,0:T(8,128)(2,1)S(1)} %bitcast_dynamic-update-slice_fusion), channel_id=1, replica_groups=mesh['grp'=4,'mem'=8] {'mem'}, dimensions={0} | all-to-all | bytes 12582912 | tf_op jit(solution)/shard_map/all_to_all | solution.py:15
  179.8 0.0 slice-done
  179.8 8.2 %fusion = f32[384,1024]{1,0:T(8,128)} fusion(bf16[384,8192]{1,0:T(8,128)(2,1)S(1)} %bitcast.22, bf16[8192,1024]{1,0:T(8,128)(2,1)S(1)} %bitcast.24, s32[1024]{0:T(1024)S(1)} %copy-done.1, s32[8192]{0:T(1024)S(1)} %copy-done), kind=kOutput, calls=%fused_computation.1 | convolution fusion | flops 6459228160 | bytes 24678400 | tf_op jit(solution)/shard_map/dot_general | solution.py:18
  188.0 0.0 reduce-scatter.3.cloned.1.call-update
  188.0 0.0 reduce-scatter.5.cloned.1.call-start
  188.1 64.6 %reduce-scatter.3.cloned.1.call-done = f32[48,1024]{1,0:T(8,128)} async-done(((f32[384,1024]{1,0:T(8,128)}), f32[48,1024]{1,0:T(8,128)}) %reduce-scatter.3.cloned.1.call-update) | async-done | bytes 196624 | tf_op jit(solution)/shard_map/reduce_scatter | solution.py:21
  252.7 0.0 reduce-scatter.5.cloned.1.call-update
  252.7 21.0 %reduce-scatter.5.cloned.1.call-done = f32[48,256]{1,0:T(8,128)} async-done(((f32[48,1024]{1,0:T(8,128)}), f32[48,256]{1,0:T(8,128)}) %reduce-scatter.5.cloned.1.call-update) | async-done | bytes 49168 | tf_op jit(solution)/shard_map/reduce_scatter | solution.py:22
  (7 shorter events, 0.0 us)
Async XLA Ops:
  6.5 246.2 %reduce-scatter.3.cloned.1.call-start = ((), (), s32[]{:S(2)}) async-start(), calls=%async_computation.3 | async-start | bytes 1769472 | tf_op jit(solution)/shard_map/reduce_scatter | solution.py:21
  27.3 152.5 %slice-start = ((s8[16777216]{0:T(1024)(128)(4,1)}), s8[4194304]{0:T(1024)(128)(4,1)S(1)}, s32[]{:S(2)}) async-start(s8[16777216]{0:T(1024)(128)(4,1)} %bitcast.23), calls=%async_computation.5 | async-start | bytes 8388608
  29.9 149.9 %slice-start.1 = ((s8[16777216]{0:T(1024)(128)(4,1)}), s8[4194304]{0:T(1024)(128)(4,1)S(1)}, s32[]{:S(2)}) async-start(s8[16777216]{0:T(1024)(128)(4,1)} %bitcast.23), calls=%async_computation.6 | async-start | bytes 8388608
  32.5 147.3 %slice-start.2 = ((s8[16777216]{0:T(1024)(128)(4,1)}), s8[4194304]{0:T(1024)(128)(4,1)S(1)}, s32[]{:S(2)}) async-start(s8[16777216]{0:T(1024)(128)(4,1)} %bitcast.23), calls=%async_computation.7 | async-start | bytes 8388608
  34.3 145.5 %slice-start.3 = ((s8[16777216]{0:T(1024)(128)(4,1)}), s8[4194304]{0:T(1024)(128)(4,1)S(1)}, s32[]{:S(2)}) async-start(s8[16777216]{0:T(1024)(128)(4,1)} %bitcast.23), calls=%async_computation.8 | async-start | bytes 8388608
  34.3 145.5 %copy-start = (s32[8192]{0:T(1024)S(1)}, s32[8192]{0:T(1024)}, u32[]{:S(2)}) copy-start(s32[8192]{0:T(1024)} %param.6) | copy-start | bytes 98308
  34.3 145.5 %copy-start.1 = (s32[1024]{0:T(1024)S(1)}, s32[1024]{0:T(1024)}, u32[]{:S(2)}) copy-start(s32[1024]{0:T(1024)} %param.7) | copy-start | bytes 12292
  188.0 85.7 %reduce-scatter.5.cloned.1.call-start = ((), (), s32[]{:S(2)}) async-start(), calls=%async_computation.4 | async-start | bytes 245760 | tf_op jit(solution)/shard_map/reduce_scatter | solution.py:22
Sparse Core Ops, SparseCore 0:
  188.2 64.5 reduce-scatter.2
  255.2 18.5 reduce-scatter.4
